TPU v7x, 32 devices: a whole 2x2x4 slice. The times are simulated.
32 devices in a mesh: node: 8 (over z, x), feat: 4 (over y, core).
Axes of the slice: x: 2, y: 2, z: 4, core: 2. Of those that a mesh axis runs over, the one named last changes fastest.
Arguments:
- features: bfloat16 [256, 4096], P('feat', 'node'), may hold values from -6 to 6
- tile_values: bfloat16 [256, 128, 128], P('node'), may hold values from -0.1875 to 0.1875
- tile_rows: int32 [64, 4], P('node'), may hold values from 0 to 3
- tile_cols: int32 [64, 4], P('node'), may hold values from 0 to 3
- tile_counts: int32 [64], P('node'), may hold values from 0 to 4, as said below
- weight: bfloat16 [256, 256], replicated, may hold values from -0.375 to 0.375
- cotangent: bfloat16 [256, 4096], P(None, ('node', 'feat')), may hold values from -6 to 6
Outputs:
- activated: bfloat16 [256, 4096], P(None, ('node', 'feat'))
- grad_weight: float32 [256, 256], replicated
- grad_features: float32 [256, 4096], P('feat', 'node')
Inputs may be any that keep to these rules, and one draw needn't show every extreme that they name: `tile_counts`: slots at or past a pair's count are ignored; some pair has all 4 slots live, and the live slots of one receiving node index vary strongly between indices.
All inputs are finite; a program needn't handle non-finite values.
Results may differ from a plain program's by a relative error of at most 0.012.
Values may be sent and summed in bfloat16 or wider, within the bound.
No kernel may reach another device: no remote copies, remote signals or barrier semaphores. Data moves between devices by JAX's collectives and lax.ppermute only.
A program may use at most 64 MiB of HBM per device.

v0:
```python
import jax
import jax.numpy as jnp
from jax import lax
from jax.sharding import PartitionSpec as P


def passed_along(x, axis, by):
    count = lax.axis_size(axis)
    return lax.ppermute(x, axis, [(i, (i + by) % count) for i in range(count)])


def select_pair(tile_values, tile_rows, tile_cols, tile_counts, source):
    slots = tile_rows.shape[1]
    values = lax.dynamic_slice_in_dim(tile_values, source * slots, slots, 0)
    row_ids = lax.dynamic_index_in_dim(tile_rows, source, 0, keepdims=False)
    col_ids = lax.dynamic_index_in_dim(tile_cols, source, 0, keepdims=False)
    number = lax.dynamic_index_in_dim(tile_counts, source, 0, keepdims=False)
    live = (jnp.arange(slots) < number).astype(jnp.float32)
    return (values, row_ids, col_ids, live)


def add_forward(totals, piece, parts, keep):
    values, row_ids, col_ids, live = parts
    blocks_in = piece.reshape(piece.shape[0], -1, values.shape[1])
    block_count = blocks_in.shape[1]
    pick = jax.nn.one_hot(col_ids, block_count, dtype=jnp.bfloat16)
    chosen = jnp.einsum("frm,sr->fsm", blocks_in, pick, preferred_element_type=jnp.float32).astype(
        jnp.bfloat16
    )
    product = jnp.einsum("fsm,sjm->fsj", chosen, values, preferred_element_type=jnp.float32)
    place = jax.nn.one_hot(row_ids, block_count, dtype=jnp.float32) * (live * keep)[:, None]
    return totals + jnp.einsum("fsj,sr->frj", product, place)


def add_backward(totals, grad_blocks, parts, keep):
    values, row_ids, col_ids, live = parts
    block_count = grad_blocks.shape[1]
    pick = jax.nn.one_hot(row_ids, block_count, dtype=jnp.bfloat16)
    chosen = jnp.einsum(
        "frj,sr->fsj", grad_blocks, pick, preferred_element_type=jnp.float32
    ).astype(jnp.bfloat16)
    product = jnp.einsum("fsj,sjm->fsm", chosen, values, preferred_element_type=jnp.float32)
    place = jax.nn.one_hot(col_ids, block_count, dtype=jnp.float32) * (live * keep)[:, None]
    return totals + jnp.einsum("fsm,sc->fcm", product, place)


def per_device(features, tile_values, tile_rows, tile_cols, tile_counts, weight, cotangent):
    node_count = lax.axis_size("node")
    own_index = lax.axis_index("node")
    slice_width = features.shape[0]
    local_nodes = features.shape[1]
    tile_side = tile_values.shape[1]
    block_count = local_nodes // tile_side

    def pair_of(source):
        return select_pair(tile_values, tile_rows, tile_cols, tile_counts, source)

    totals = jnp.zeros((slice_width, block_count, tile_side), jnp.float32)
    totals = add_forward(totals, features, pair_of(own_index), 1.0)

    def ahead_step(step, carry):
        running, moving = carry
        moving = passed_along(moving, "node", 1)
        source = (own_index - step) % node_count
        return (add_forward(running, moving, pair_of(source), 1.0), moving)

    totals, _ = lax.fori_loop(1, node_count, ahead_step, (totals, features))
    aggregated = totals.reshape(slice_width, local_nodes).astype(jnp.bfloat16)
    full_rows = lax.all_to_all(aggregated, "feat", split_axis=1, concat_axis=0, tiled=True)
    pre = jnp.dot(weight.T, full_rows, preferred_element_type=jnp.float32)
    activated = jax.nn.silu(pre).astype(jnp.bfloat16)
    sigma = jax.nn.sigmoid(pre)
    dpre = (cotangent.astype(jnp.float32) * sigma * (1.0 + pre * (1.0 - sigma))).astype(
        jnp.bfloat16
    )
    weight_part = lax.dot_general(
        full_rows, dpre, (((1,), (1,)), ((), ())), preferred_element_type=jnp.float32
    )
    grad_weight = lax.psum(weight_part, ("node", "feat"))
    dagg = jnp.dot(weight, dpre, preferred_element_type=jnp.float32).astype(jnp.bfloat16)
    grad_slices = lax.all_to_all(dagg, "feat", split_axis=0, concat_axis=1, tiled=True)
    grad_blocks = grad_slices.reshape(slice_width, block_count, tile_side)
    zeros = jnp.zeros((slice_width, block_count, tile_side), jnp.float32)
    start = add_backward(zeros, grad_blocks, pair_of((own_index - 1) % node_count), 1.0)

    def carry_step(step, running):
        running = passed_along(running, "node", 1)
        owner = (own_index - step - 1) % node_count
        return add_backward(running, grad_blocks, pair_of(owner), 1.0)

    gradient = lax.fori_loop(1, node_count, carry_step, start)
    return (activated, grad_weight, gradient.reshape(slice_width, local_nodes))


def solution(mesh):
    placed = (
        P("feat", "node"),
        P("node", None, None),
        P("node", None),
        P("node", None),
        P("node"),
        P(),
        P(None, ("node", "feat")),
    )
    return jax.shard_map(
        per_device,
        mesh=mesh,
        in_specs=placed,
        out_specs=(P(None, ("node", "feat")), P(), P("feat", "node")),
        check_vma=False,
    )
```

profile of v0, /device:TPU:0, one launch (start us, length us, event | category | flops | bytes accessed | tf_op | source)
XLA Modules:
  0.0 227.0 jit_solution(9543807741233657913)
XLA Ops:
  7.2 0.9 copy.98
  8.1 0.7 copy-done.2
  11.7 1.1 fusion.47
  12.9 62.7 %while.32 = (s32[]{:T(128)}, f32[64,4,128]{2,1,0:T(4,128)S(1)}, bf16[64,512]{1,0:T(8,128)(2,1)S(1)}, s32[]{:T(128)}, s32[8,4]{1,0:T(8,128)S(1)}, /*index=5*/s32[...) while((s32[]{:T(128)}, f32[64,4,128]{2,1,0:T(4,128)S(1)}, ...), condition=%wide.region_1.2_spmd, body=%wide.region_0.1_spmd.sunk | while | flops 8945741 | bytes 1245694 | solution.py:67
  12.9 3.0 %collective-permute-start = (bf16[64,512]{1,0:T(8,128)(2,1)S(1)}, bf16[64,512]{1,0:T(8,128)(2,1)S(1)}, u32[]{:S(2)}, u32[]{:S(2)}) collective-permute-start(bf16[64,512]{1,0:T(8,128)(2,1)S(1)} %get-tuple-element.610), channel_id=1, source_target_pairs={{0,4},{4,8},{8,12},{12,16},{16,20},{20,24},{24,28},{28,0},{1,5},{5... | collective-permute-start | bytes 196616 | tf_op jit(solution)/shard_map/while/body/eval_jaxpr/ppermute | solution.py:9
  17.2 4.0 %collective-permute-done = bf16[64,512]{1,0:T(8,128)(2,1)S(1)} collective-permute-done((bf16[64,512]{1,0:T(8,128)(2,1)S(1)}, bf16[64,512]{1,0:T(8,128)(2,1)S(1)}, u32[]{:S(2)}, u32[]{:S(2)}) %collective-permute-start) | collective-permute-done | bytes 65568 | tf_op jit(solution)/shard_map/while/body/eval_jaxpr/ppermute | solution.py:9
  21.5 1.1 fusion.115
  24.3 5.7 %collective-permute-done = bf16[64,512]{1,0:T(8,128)(2,1)S(1)} collective-permute-done((bf16[64,512]{1,0:T(8,128)(2,1)S(1)}, bf16[64,512]{1,0:T(8,128)(2,1)S(1)}, u32[]{:S(2)}, u32[]{:S(2)}) %collective-permute-start) | collective-permute-done | bytes 65568 | tf_op jit(solution)/shard_map/while/body/eval_jaxpr/ppermute | solution.py:9
  30.3 1.1 fusion.115
  33.1 5.7 %collective-permute-done = bf16[64,512]{1,0:T(8,128)(2,1)S(1)} collective-permute-done((bf16[64,512]{1,0:T(8,128)(2,1)S(1)}, bf16[64,512]{1,0:T(8,128)(2,1)S(1)}, u32[]{:S(2)}, u32[]{:S(2)}) %collective-permute-start) | collective-permute-done | bytes 65568 | tf_op jit(solution)/shard_map/while/body/eval_jaxpr/ppermute | solution.py:9
  39.0 1.1 fusion.115
  41.9 5.7 %collective-permute-done = bf16[64,512]{1,0:T(8,128)(2,1)S(1)} collective-permute-done((bf16[64,512]{1,0:T(8,128)(2,1)S(1)}, bf16[64,512]{1,0:T(8,128)(2,1)S(1)}, u32[]{:S(2)}, u32[]{:S(2)}) %collective-permute-start) | collective-permute-done | bytes 65568 | tf_op jit(solution)/shard_map/while/body/eval_jaxpr/ppermute | solution.py:9
  47.8 1.1 fusion.115
  50.6 5.7 %collective-permute-done = bf16[64,512]{1,0:T(8,128)(2,1)S(1)} collective-permute-done((bf16[64,512]{1,0:T(8,128)(2,1)S(1)}, bf16[64,512]{1,0:T(8,128)(2,1)S(1)}, u32[]{:S(2)}, u32[]{:S(2)}) %collective-permute-start) | collective-permute-done | bytes 65568 | tf_op jit(solution)/shard_map/while/body/eval_jaxpr/ppermute | solution.py:9
  56.6 1.1 fusion.115
  59.4 5.7 %collective-permute-done = bf16[64,512]{1,0:T(8,128)(2,1)S(1)} collective-permute-done((bf16[64,512]{1,0:T(8,128)(2,1)S(1)}, bf16[64,512]{1,0:T(8,128)(2,1)S(1)}, u32[]{:S(2)}, u32[]{:S(2)}) %collective-permute-start) | collective-permute-done | bytes 65568 | tf_op jit(solution)/shard_map/while/body/eval_jaxpr/ppermute | solution.py:9
  65.3 1.1 fusion.115
  68.2 5.7 %collective-permute-done = bf16[64,512]{1,0:T(8,128)(2,1)S(1)} collective-permute-done((bf16[64,512]{1,0:T(8,128)(2,1)S(1)}, bf16[64,512]{1,0:T(8,128)(2,1)S(1)}, u32[]{:S(2)}, u32[]{:S(2)}) %collective-permute-start) | collective-permute-done | bytes 65568 | tf_op jit(solution)/shard_map/while/body/eval_jaxpr/ppermute | solution.py:9
  74.1 1.1 fusion.115
  76.2 3.4 %all-to-all-start = ((bf16[64,4,128]{2,0,1:T(8,128)(2,1)}), bf16[64,4,128]{2,0,1:T(8,128)(2,1)S(1)}, u32[]{:S(2)}, u32[]{:S(2)}) async-start(bf16[64,4,128]{2,0,1:T(8,128)(2,1)} %copy.71), calls=%async_computation | async-start | bytes 131072 | tf_op jit(solution)/shard_map/all_to_all | solution.py:69
  79.7 0.7 compare_convert_fusion.2
  80.5 3.3 %all-to-all-done = bf16[64,4,128]{2,0,1:T(8,128)(2,1)S(1)} async-done(((bf16[64,4,128]{2,0,1:T(8,128)(2,1)}), bf16[64,4,128]{2,0,1:T(8,128)(2,1)S(1)}, u32[]{:S(2)}, u32[]{:S(2)}) %all-to-all-start) | async-done | bytes 65568 | tf_op jit(solution)/shard_map/all_to_all | solution.py:69
  84.2 0.7 copy.21
  84.9 3.3 %all-to-all-start.1 = ((bf16[4,64,128]{2,1,0:T(8,128)(2,1)}), bf16[4,64,128]{2,1,0:T(8,128)(2,1)S(1)}, u32[]{:S(2)}, u32[]{:S(2)}) async-start(bf16[4,64,128]{2,1,0:T(8,128)(2,1)} %bitcast.30), calls=%async_computation.1 | async-start | bytes 131072 | tf_op jit(solution)/shard_map/all_to_all | solution.py:81
  88.3 0.9 fusion.77
  89.2 0.7 copy.25
  89.9 2.4 %all-to-all-done.1 = bf16[4,64,128]{2,1,0:T(8,128)(2,1)S(1)} async-done(((bf16[4,64,128]{2,1,0:T(8,128)(2,1)}), bf16[4,64,128]{2,1,0:T(8,128)(2,1)S(1)}, u32[]{:S(2)}, u32[]{:S(2)}) %all-to-all-start.1) | async-done | bytes 65568 | tf_op jit(solution)/shard_map/all_to_all | solution.py:81
  92.6 1.1 fusion.45
  93.9 58.6 %while.33 = (s32[]{:T(128)}, f32[64,4,128]{2,1,0:T(4,128)S(1)}, s32[]{:T(128)}, s32[8,4]{1,0:T(8,128)S(1)}, s32[8]{0:T(128)S(1)}, /*index=5*/bf16[32,128,128]{2,...) while((s32[]{:T(128)}, f32[64,4,128]{2,1,0:T(4,128)S(1)}, ...), condition=%wide.region_4.5_spmd, body=%wide.region_3.4_spmd.sunk | while | flops 8945742 | bytes 1245714 | solution.py:91
  94.2 1.1 fusion.125
  96.5 5.2 %collective-permute-done.1 = f32[64,4,128]{2,1,0:T(4,128)S(1)} collective-permute-done((f32[64,4,128]{2,1,0:T(4,128)S(1)}, f32[64,4,128]{2,1,0:T(4,128)S(1)}, u32[]{:S(2)}, u32[]{:S(2)}) %collective-permute-start.1) | collective-permute-done | bytes 131104 | tf_op jit(solution)/shard_map/while/body/eval_jaxpr/ppermute | solution.py:9
  102.5 1.1 fusion.125
  104.8 5.2 %collective-permute-done.1 = f32[64,4,128]{2,1,0:T(4,128)S(1)} collective-permute-done((f32[64,4,128]{2,1,0:T(4,128)S(1)}, f32[64,4,128]{2,1,0:T(4,128)S(1)}, u32[]{:S(2)}, u32[]{:S(2)}) %collective-permute-start.1) | collective-permute-done | bytes 131104 | tf_op jit(solution)/shard_map/while/body/eval_jaxpr/ppermute | solution.py:9
  110.7 1.1 fusion.125
  112.4 0.6 compare_convert_fusion.7
  113.0 5.2 %collective-permute-done.1 = f32[64,4,128]{2,1,0:T(4,128)S(1)} collective-permute-done((f32[64,4,128]{2,1,0:T(4,128)S(1)}, f32[64,4,128]{2,1,0:T(4,128)S(1)}, u32[]{:S(2)}, u32[]{:S(2)}) %collective-permute-start.1) | collective-permute-done | bytes 131104 | tf_op jit(solution)/shard_map/while/body/eval_jaxpr/ppermute | solution.py:9
  118.9 1.1 fusion.125
  120.6 0.6 compare_convert_fusion.7
  121.2 5.1 %collective-permute-done.1 = f32[64,4,128]{2,1,0:T(4,128)S(1)} collective-permute-done((f32[64,4,128]{2,1,0:T(4,128)S(1)}, f32[64,4,128]{2,1,0:T(4,128)S(1)}, u32[]{:S(2)}, u32[]{:S(2)}) %collective-permute-start.1) | collective-permute-done | bytes 131104 | tf_op jit(solution)/shard_map/while/body/eval_jaxpr/ppermute | solution.py:9
  127.0 1.1 fusion.125
  129.3 5.3 %collective-permute-done.1 = f32[64,4,128]{2,1,0:T(4,128)S(1)} collective-permute-done((f32[64,4,128]{2,1,0:T(4,128)S(1)}, f32[64,4,128]{2,1,0:T(4,128)S(1)}, u32[]{:S(2)}, u32[]{:S(2)}) %collective-permute-start.1) | collective-permute-done | bytes 131104 | tf_op jit(solution)/shard_map/while/body/eval_jaxpr/ppermute | solution.py:9
  135.4 1.1 fusion.125
  137.7 6.3 %collective-permute-done.1 = f32[64,4,128]{2,1,0:T(4,128)S(1)} collective-permute-done((f32[64,4,128]{2,1,0:T(4,128)S(1)}, f32[64,4,128]{2,1,0:T(4,128)S(1)}, u32[]{:S(2)}, u32[]{:S(2)}) %collective-permute-start.1) | collective-permute-done | bytes 131104 | tf_op jit(solution)/shard_map/while/body/eval_jaxpr/ppermute | solution.py:9
  144.7 1.1 fusion.125
  147.0 5.2 %collective-permute-done.1 = f32[64,4,128]{2,1,0:T(4,128)S(1)} collective-permute-done((f32[64,4,128]{2,1,0:T(4,128)S(1)}, f32[64,4,128]{2,1,0:T(4,128)S(1)}, u32[]{:S(2)}, u32[]{:S(2)}) %collective-permute-start.1) | collective-permute-done | bytes 131104 | tf_op jit(solution)/shard_map/while/body/eval_jaxpr/ppermute | solution.py:9
  152.5 0.7 copy.72
  153.2 65.3 %all-reduce.2.cloned.1.call-done = f32[256,256]{1,0:T(8,128)} async-done(((f32[256,256]{1,0:T(8,128)}), f32[256,256]{1,0:T(8,128)}) %all-reduce.2.cloned.1.call-update) | async-done | bytes 262160 | tf_op jit(solution)/shard_map/psum | solution.py:79
  218.5 1.7 copy.99
  (121 shorter events, 30.4 us)
Async XLA Ops:
  7.2 76.6 %copy-start = (bf16[256,256]{1,0:T(8,128)(2,1)S(1)}, bf16[256,256]{1,0:T(8,128)(2,1)}, u32[]{:S(2)}) copy-start(bf16[256,256]{1,0:T(8,128)(2,1)} %param.16) | copy-start | bytes 393220
  8.1 0.7 copy-start.2
  8.7 0.7 copy-start.3
  9.5 0.7 copy-start.4
  12.9 8.3 %collective-permute-start = (bf16[64,512]{1,0:T(8,128)(2,1)S(1)}, bf16[64,512]{1,0:T(8,128)(2,1)S(1)}, u32[]{:S(2)}, u32[]{:S(2)}) collective-permute-start(bf16[64,512]{1,0:T(8,128)(2,1)S(1)} %get-tuple-element.610), channel_id=1, source_target_pairs={{0,4},{4,8},{8,12},{12,16},{16,20},{20,24},{24,28},{28,0},{1,5},{5... | collective-permute-start | bytes 196616 | tf_op jit(solution)/shard_map/while/body/eval_jaxpr/ppermute | solution.py:9
  23.0 7.0 %collective-permute-start = (bf16[64,512]{1,0:T(8,128)(2,1)S(1)}, bf16[64,512]{1,0:T(8,128)(2,1)S(1)}, u32[]{:S(2)}, u32[]{:S(2)}) collective-permute-start(bf16[64,512]{1,0:T(8,128)(2,1)S(1)} %get-tuple-element.610), channel_id=1, source_target_pairs={{0,4},{4,8},{8,12},{12,16},{16,20},{20,24},{24,28},{28,0},{1,5},{5... | collective-permute-start | bytes 196616 | tf_op jit(solution)/shard_map/while/body/eval_jaxpr/ppermute | solution.py:9
  31.7 7.0 %collective-permute-start = (bf16[64,512]{1,0:T(8,128)(2,1)S(1)}, bf16[64,512]{1,0:T(8,128)(2,1)S(1)}, u32[]{:S(2)}, u32[]{:S(2)}) collective-permute-start(bf16[64,512]{1,0:T(8,128)(2,1)S(1)} %get-tuple-element.610), channel_id=1, source_target_pairs={{0,4},{4,8},{8,12},{12,16},{16,20},{20,24},{24,28},{28,0},{1,5},{5... | collective-permute-start | bytes 196616 | tf_op jit(solution)/shard_map/while/body/eval_jaxpr/ppermute | solution.py:9
  40.5 7.0 %collective-permute-start = (bf16[64,512]{1,0:T(8,128)(2,1)S(1)}, bf16[64,512]{1,0:T(8,128)(2,1)S(1)}, u32[]{:S(2)}, u32[]{:S(2)}) collective-permute-start(bf16[64,512]{1,0:T(8,128)(2,1)S(1)} %get-tuple-element.610), channel_id=1, source_target_pairs={{0,4},{4,8},{8,12},{12,16},{16,20},{20,24},{24,28},{28,0},{1,5},{5... | collective-permute-start | bytes 196616 | tf_op jit(solution)/shard_map/while/body/eval_jaxpr/ppermute | solution.py:9
  49.3 7.0 %collective-permute-start = (bf16[64,512]{1,0:T(8,128)(2,1)S(1)}, bf16[64,512]{1,0:T(8,128)(2,1)S(1)}, u32[]{:S(2)}, u32[]{:S(2)}) collective-permute-start(bf16[64,512]{1,0:T(8,128)(2,1)S(1)} %get-tuple-element.610), channel_id=1, source_target_pairs={{0,4},{4,8},{8,12},{12,16},{16,20},{20,24},{24,28},{28,0},{1,5},{5... | collective-permute-start | bytes 196616 | tf_op jit(solution)/shard_map/while/body/eval_jaxpr/ppermute | solution.py:9
  58.1 7.0 %collective-permute-start = (bf16[64,512]{1,0:T(8,128)(2,1)S(1)}, bf16[64,512]{1,0:T(8,128)(2,1)S(1)}, u32[]{:S(2)}, u32[]{:S(2)}) collective-permute-start(bf16[64,512]{1,0:T(8,128)(2,1)S(1)} %get-tuple-element.610), channel_id=1, source_target_pairs={{0,4},{4,8},{8,12},{12,16},{16,20},{20,24},{24,28},{28,0},{1,5},{5... | collective-permute-start | bytes 196616 | tf_op jit(solution)/shard_map/while/body/eval_jaxpr/ppermute | solution.py:9
  66.8 7.0 %collective-permute-start = (bf16[64,512]{1,0:T(8,128)(2,1)S(1)}, bf16[64,512]{1,0:T(8,128)(2,1)S(1)}, u32[]{:S(2)}, u32[]{:S(2)}) collective-permute-start(bf16[64,512]{1,0:T(8,128)(2,1)S(1)} %get-tuple-element.610), channel_id=1, source_target_pairs={{0,4},{4,8},{8,12},{12,16},{16,20},{20,24},{24,28},{28,0},{1,5},{5... | collective-permute-start | bytes 196616 | tf_op jit(solution)/shard_map/while/body/eval_jaxpr/ppermute | solution.py:9
  76.2 4.1 %copy-start.1 = (bf16[256,128]{1,0:T(8,128)(2,1)S(1)}, bf16[256,128]{1,0:T(8,128)(2,1)}, u32[]{:S(2)}) copy-start(bf16[256,128]{1,0:T(8,128)(2,1)} %param.17) | copy-start | bytes 196612
  76.2 7.5 %all-to-all-start = ((bf16[64,4,128]{2,0,1:T(8,128)(2,1)}), bf16[64,4,128]{2,0,1:T(8,128)(2,1)S(1)}, u32[]{:S(2)}, u32[]{:S(2)}) async-start(bf16[64,4,128]{2,0,1:T(8,128)(2,1)} %copy.71), calls=%async_computation | async-start | bytes 131072 | tf_op jit(solution)/shard_map/all_to_all | solution.py:69
  84.9 7.4 %all-to-all-start.1 = ((bf16[4,64,128]{2,1,0:T(8,128)(2,1)}), bf16[4,64,128]{2,1,0:T(8,128)(2,1)S(1)}, u32[]{:S(2)}, u32[]{:S(2)}) async-start(bf16[4,64,128]{2,1,0:T(8,128)(2,1)} %bitcast.30), calls=%async_computation.1 | async-start | bytes 131072 | tf_op jit(solution)/shard_map/all_to_all | solution.py:81
  88.2 130.3 %all-reduce.2.cloned.1.call-start = ((), (), s32[]{:S(2)}) async-start(), calls=%async_computation.2 | async-start | bytes 524288 | tf_op jit(solution)/shard_map/psum | solution.py:79
  93.9 7.9 %collective-permute-start.1 = (f32[64,4,128]{2,1,0:T(4,128)S(1)}, f32[64,4,128]{2,1,0:T(4,128)S(1)}, u32[]{:S(2)}, u32[]{:S(2)}) collective-permute-start(f32[64,4,128]{2,1,0:T(4,128)S(1)} %get-tuple-element.652), channel_id=1, source_target_pairs={{0,4},{4,8},{8,12},{12,16},{16,20},{20,24},{24,28},{28,0},{1,5},{5... | collective-permute-start | bytes 393224 | tf_op jit(solution)/shard_map/while/body/eval_jaxpr/ppermute | solution.py:9
  102.1 7.9 %collective-permute-start.1 = (f32[64,4,128]{2,1,0:T(4,128)S(1)}, f32[64,4,128]{2,1,0:T(4,128)S(1)}, u32[]{:S(2)}, u32[]{:S(2)}) collective-permute-start(f32[64,4,128]{2,1,0:T(4,128)S(1)} %get-tuple-element.652), channel_id=1, source_target_pairs={{0,4},{4,8},{8,12},{12,16},{16,20},{20,24},{24,28},{28,0},{1,5},{5... | collective-permute-start | bytes 393224 | tf_op jit(solution)/shard_map/while/body/eval_jaxpr/ppermute | solution.py:9
  110.4 7.9 %collective-permute-start.1 = (f32[64,4,128]{2,1,0:T(4,128)S(1)}, f32[64,4,128]{2,1,0:T(4,128)S(1)}, u32[]{:S(2)}, u32[]{:S(2)}) collective-permute-start(f32[64,4,128]{2,1,0:T(4,128)S(1)} %get-tuple-element.652), channel_id=1, source_target_pairs={{0,4},{4,8},{8,12},{12,16},{16,20},{20,24},{24,28},{28,0},{1,5},{5... | collective-permute-start | bytes 393224 | tf_op jit(solution)/shard_map/while/body/eval_jaxpr/ppermute | solution.py:9
  118.6 7.7 %collective-permute-start.1 = (f32[64,4,128]{2,1,0:T(4,128)S(1)}, f32[64,4,128]{2,1,0:T(4,128)S(1)}, u32[]{:S(2)}, u32[]{:S(2)}) collective-permute-start(f32[64,4,128]{2,1,0:T(4,128)S(1)} %get-tuple-element.652), channel_id=1, source_target_pairs={{0,4},{4,8},{8,12},{12,16},{16,20},{20,24},{24,28},{28,0},{1,5},{5... | collective-permute-start | bytes 393224 | tf_op jit(solution)/shard_map/while/body/eval_jaxpr/ppermute | solution.py:9
  126.7 8.0 %collective-permute-start.1 = (f32[64,4,128]{2,1,0:T(4,128)S(1)}, f32[64,4,128]{2,1,0:T(4,128)S(1)}, u32[]{:S(2)}, u32[]{:S(2)}) collective-permute-start(f32[64,4,128]{2,1,0:T(4,128)S(1)} %get-tuple-element.652), channel_id=1, source_target_pairs={{0,4},{4,8},{8,12},{12,16},{16,20},{20,24},{24,28},{28,0},{1,5},{5... | collective-permute-start | bytes 393224 | tf_op jit(solution)/shard_map/while/body/eval_jaxpr/ppermute | solution.py:9
  135.0 8.9 %collective-permute-start.1 = (f32[64,4,128]{2,1,0:T(4,128)S(1)}, f32[64,4,128]{2,1,0:T(4,128)S(1)}, u32[]{:S(2)}, u32[]{:S(2)}) collective-permute-start(f32[64,4,128]{2,1,0:T(4,128)S(1)} %get-tuple-element.652), channel_id=1, source_target_pairs={{0,4},{4,8},{8,12},{12,16},{16,20},{20,24},{24,28},{28,0},{1,5},{5... | collective-permute-start | bytes 393224 | tf_op jit(solution)/shard_map/while/body/eval_jaxpr/ppermute | solution.py:9
  144.3 7.8 %collective-permute-start.1 = (f32[64,4,128]{2,1,0:T(4,128)S(1)}, f32[64,4,128]{2,1,0:T(4,128)S(1)}, u32[]{:S(2)}, u32[]{:S(2)}) collective-permute-start(f32[64,4,128]{2,1,0:T(4,128)S(1)} %get-tuple-element.652), channel_id=1, source_target_pairs={{0,4},{4,8},{8,12},{12,16},{16,20},{20,24},{24,28},{28,0},{1,5},{5... | collective-permute-start | bytes 393224 | tf_op jit(solution)/shard_map/while/body/eval_jaxpr/ppermute | solution.py:9
Sparse Core Ops, SparseCore 0:
  95.1 123.3 all-reduce.1
where the time goes:
time: 228 us; the launch traced here: 227 us
  waiting for transfers between devices  147 us (64%)
  matrix products  27.7 us (12%)
  local copies, waits for them, and re-layouts  16.8 us (7%)
  between operations  14.2 us (6%)
  starting transfers between devices  10.5 us (5%)
  other arithmetic  10.4 us (5%)
    ppermute x14, waiting for transfers between devices, passed_along(): return lax.ppermute(x, axis, [(i, (i + by) % count) for i in range(count)])  75.5 us
    psum x1, waiting for transfers between devices, per_device(): grad_weight = lax.psum(weight_part, ('node', 'feat'))  65.3 us
    convert_element_type x16, other arithmetic, select_pair(): live = (jnp.arange(slots) < number).astype(jnp.float32)  10.4 us
    dynamic_slice x15, local copies, waits for them, and re-layouts, select_pair(): number = lax.dynamic_index_in_dim(tile_counts, source, 0, keepdims=False)  8.87 us
    dot_general x8, matrix products, add_forward(): jnp.einsum('fsm,sjm->fsj', chosen, values, preferred_element_type=jnp.flo...  8.64 us
    dot_general x8, matrix products, add_backward(): jnp.einsum('fsj,sjm->fsm', chosen, values, preferred_element_type=jnp.flo...  8.47 us
    unnamed x15, local copies, waits for them, and re-layouts  5.78 us
  transfers between devices with their start and end apart: 17, of which 17 were waited for; matrix products, arithmetic and copies ran while one was open for 15% of the time, Pallas kernels for 0%

commit v1 on v0

--- a/solution.py
+++ b/solution.py
@@ -2,6 +2,19 @@
 import jax.numpy as jnp
 from jax import lax
 from jax.sharding import PartitionSpec as P
+
+
+def _answer_members_all(page, array_dim, local_values):
+    value_now, state_now = (page.shape[:array_dim], page.shape[array_dim + 1 :])
+    reply = jnp.moveaxis(page.reshape(*value_now, local_values, -1, *state_now), array_dim, 0)
+    return reply
+
+
+def loops_draw(slab_in, axis_k):
+    r_now = list(slab_in.shape[1:])
+    r_now[axis_k] *= slab_in.shape[0]
+    arr_out = jnp.moveaxis(slab_in, 0, axis_k).reshape(r_now)
+    return arr_out
 
 
 def passed_along(x, axis, by):
@@ -78,7 +91,16 @@
     )
     grad_weight = lax.psum(weight_part, ("node", "feat"))
     dagg = jnp.dot(weight, dpre, preferred_element_type=jnp.float32).astype(jnp.bfloat16)
-    grad_slices = lax.all_to_all(dagg, "feat", split_axis=0, concat_axis=1, tiled=True)
+    a_next, o_now = (lax.axis_size("feat"), lax.axis_index("feat"))
+    even = _answer_members_all(dagg, 0, a_next)
+    log = [even[o_now]]
+    j = 1
+    while j < a_next:
+        carry_out = even[o_now ^ j]
+        log.append(lax.ppermute(carry_out, "feat", [(i0, i0 ^ j) for i0 in range(a_next)]))
+        j = j + 1
+    even = jnp.stack(log)[o_now ^ jnp.arange(a_next)]
+    grad_slices = loops_draw(even, 1)
     grad_blocks = grad_slices.reshape(slice_width, block_count, tile_side)
     zeros = jnp.zeros((slice_width, block_count, tile_side), jnp.float32)
     start = add_backward(zeros, grad_blocks, pair_of((own_index - 1) % node_count), 1.0)

time: 228 us -> 220 us (0.965)
  waiting for transfers between devices: 147 us -> 139 us
    psum x1, waiting for transfers between devices: 65.3 us -> 60.2 us  [per_device(): grad_weight = lax.psum(weight_part, ('node', 'feat'))]
    all_to_all x1 -> x0, starting transfers between devices: 3.28 us -> none  [per_device(): lax.all_to_all(dagg, 'feat', split_axis=0, concat_axis=1, tiled=True)]
    all_to_all x1 -> x0, waiting for transfers between devices: 2.4 us -> none  [per_device(): lax.all_to_all(dagg, 'feat', split_axis=0, concat_axis=1, tiled=True)]
  transfers between devices with their start and end apart: 17 -> 19, of which waited for: 17 -> 17; matrix products, arithmetic and copies ran while one was open for 15% -> 16% of each run, Pallas kernels for 0% -> 0%
where the time goes in v1:
time: 220 us; the launch traced here: 219 us
  waiting for transfers between devices  139 us (63%)
  matrix products  27.7 us (13%)
  local copies, waits for them, and re-layouts  17.3 us (8%)
  between operations  14.3 us (6%)
  other arithmetic  10.5 us (5%)
  starting transfers between devices  9.13 us (4%)
    ppermute x14, waiting for transfers between devices, passed_along(): return lax.ppermute(x, axis, [(i, (i + by) % count) for i in range(count)])  75.1 us
    psum x1, waiting for transfers between devices, per_device(): grad_weight = lax.psum(weight_part, ('node', 'feat'))  60.2 us
    convert_element_type x16, other arithmetic, select_pair(): live = (jnp.arange(slots) < number).astype(jnp.float32)  10.5 us
    dynamic_slice x15, local copies, waits for them, and re-layouts, select_pair(): number = lax.dynamic_index_in_dim(tile_counts, source, 0, keepdims=False)  9.49 us
    dot_general x8, matrix products, add_forward(): jnp.einsum('fsm,sjm->fsj', chosen, values, preferred_element_type=jnp.flo...  8.63 us
    dot_general x8, matrix products, add_backward(): jnp.einsum('fsj,sjm->fsm', chosen, values, preferred_element_type=jnp.flo...  8.48 us
    unnamed x15, local copies, waits for them, and re-layouts  5.78 us
  transfers between devices with their start and end apart: 19, of which 17 were waited for; matrix products, arithmetic and copies ran while one was open for 16% of the time, Pallas kernels for 0%

profile of v1, /device:TPU:0, one launch (start us, length us, event | category | flops | bytes accessed | tf_op | source)
XLA Modules:
  0.0 218.8 jit_solution(77976731636377869)
XLA Ops:
  7.2 0.9 copy.97
  10.8 0.7 compare_convert_fusion.3
  11.8 1.1 fusion.47
  13.0 62.7 %while.32 = (s32[]{:T(128)}, f32[64,4,128]{2,1,0:T(4,128)S(1)}, bf16[64,512]{1,0:T(8,128)(2,1)S(1)}, s32[]{:T(128)}, s32[8,4]{1,0:T(8,128)S(1)}, /*index=5*/s32[...) while((s32[]{:T(128)}, f32[64,4,128]{2,1,0:T(4,128)S(1)}, ...), condition=%wide.region_1.2_spmd, body=%wide.region_0.1_spmd.sunk | while | flops 8945741 | bytes 1245694 | solution.py:80
  13.1 3.0 %collective-permute-start = (bf16[64,512]{1,0:T(8,128)(2,1)S(1)}, bf16[64,512]{1,0:T(8,128)(2,1)S(1)}, u32[]{:S(2)}, u32[]{:S(2)}) collective-permute-start(bf16[64,512]{1,0:T(8,128)(2,1)S(1)} %get-tuple-element.614), channel_id=1, source_target_pairs={{0,4},{4,8},{8,12},{12,16},{16,20},{20,24},{24,28},{28,0},{1,5},{5... | collective-permute-start | bytes 196616 | tf_op jit(solution)/shard_map/while/body/eval_jaxpr/ppermute | solution.py:22
  16.7 0.7 compare_convert_fusion.6
  17.4 3.9 %collective-permute-done = bf16[64,512]{1,0:T(8,128)(2,1)S(1)} collective-permute-done((bf16[64,512]{1,0:T(8,128)(2,1)S(1)}, bf16[64,512]{1,0:T(8,128)(2,1)S(1)}, u32[]{:S(2)}, u32[]{:S(2)}) %collective-permute-start) | collective-permute-done | bytes 65568 | tf_op jit(solution)/shard_map/while/body/eval_jaxpr/ppermute | solution.py:22
  21.6 1.1 fusion.120
  23.8 0.7 compare_convert_fusion.6
  24.5 5.6 %collective-permute-done = bf16[64,512]{1,0:T(8,128)(2,1)S(1)} collective-permute-done((bf16[64,512]{1,0:T(8,128)(2,1)S(1)}, bf16[64,512]{1,0:T(8,128)(2,1)S(1)}, u32[]{:S(2)}, u32[]{:S(2)}) %collective-permute-start) | collective-permute-done | bytes 65568 | tf_op jit(solution)/shard_map/while/body/eval_jaxpr/ppermute | solution.py:22
  30.4 1.1 fusion.120
  32.6 0.7 compare_convert_fusion.6
  33.3 5.6 %collective-permute-done = bf16[64,512]{1,0:T(8,128)(2,1)S(1)} collective-permute-done((bf16[64,512]{1,0:T(8,128)(2,1)S(1)}, bf16[64,512]{1,0:T(8,128)(2,1)S(1)}, u32[]{:S(2)}, u32[]{:S(2)}) %collective-permute-start) | collective-permute-done | bytes 65568 | tf_op jit(solution)/shard_map/while/body/eval_jaxpr/ppermute | solution.py:22
  39.1 1.1 fusion.120
  41.4 0.7 compare_convert_fusion.6
  42.1 5.6 %collective-permute-done = bf16[64,512]{1,0:T(8,128)(2,1)S(1)} collective-permute-done((bf16[64,512]{1,0:T(8,128)(2,1)S(1)}, bf16[64,512]{1,0:T(8,128)(2,1)S(1)}, u32[]{:S(2)}, u32[]{:S(2)}) %collective-permute-start) | collective-permute-done | bytes 65568 | tf_op jit(solution)/shard_map/while/body/eval_jaxpr/ppermute | solution.py:22
  47.9 1.1 fusion.120
  50.2 0.7 compare_convert_fusion.6
  50.8 5.6 %collective-permute-done = bf16[64,512]{1,0:T(8,128)(2,1)S(1)} collective-permute-done((bf16[64,512]{1,0:T(8,128)(2,1)S(1)}, bf16[64,512]{1,0:T(8,128)(2,1)S(1)}, u32[]{:S(2)}, u32[]{:S(2)}) %collective-permute-start) | collective-permute-done | bytes 65568 | tf_op jit(solution)/shard_map/while/body/eval_jaxpr/ppermute | solution.py:22
  56.7 1.1 fusion.120
  58.9 0.7 compare_convert_fusion.6
  59.6 5.6 %collective-permute-done = bf16[64,512]{1,0:T(8,128)(2,1)S(1)} collective-permute-done((bf16[64,512]{1,0:T(8,128)(2,1)S(1)}, bf16[64,512]{1,0:T(8,128)(2,1)S(1)}, u32[]{:S(2)}, u32[]{:S(2)}) %collective-permute-start) | collective-permute-done | bytes 65568 | tf_op jit(solution)/shard_map/while/body/eval_jaxpr/ppermute | solution.py:22
  65.4 1.1 fusion.120
  68.4 5.6 %collective-permute-done = bf16[64,512]{1,0:T(8,128)(2,1)S(1)} collective-permute-done((bf16[64,512]{1,0:T(8,128)(2,1)S(1)}, bf16[64,512]{1,0:T(8,128)(2,1)S(1)}, u32[]{:S(2)}, u32[]{:S(2)}) %collective-permute-start) | collective-permute-done | bytes 65568 | tf_op jit(solution)/shard_map/while/body/eval_jaxpr/ppermute | solution.py:22
  74.2 1.1 fusion.120
  76.3 3.4 %all-to-all-start = ((bf16[64,4,128]{2,0,1:T(8,128)(2,1)}), bf16[64,4,128]{2,0,1:T(8,128)(2,1)S(1)}, u32[]{:S(2)}, u32[]{:S(2)}) async-start(bf16[64,4,128]{2,0,1:T(8,128)(2,1)} %copy.70), calls=%async_computation | async-start | bytes 131072 | tf_op jit(solution)/shard_map/all_to_all | solution.py:82
  80.7 3.2 %all-to-all-done = bf16[64,4,128]{2,0,1:T(8,128)(2,1)S(1)} async-done(((bf16[64,4,128]{2,0,1:T(8,128)(2,1)}), bf16[64,4,128]{2,0,1:T(8,128)(2,1)S(1)}, u32[]{:S(2)}, u32[]{:S(2)}) %all-to-all-start) | async-done | bytes 65568 | tf_op jit(solution)/shard_map/all_to_all | solution.py:82
  84.5 1.3 collective-permute-start.3
  86.4 0.9 fusion.82
  87.3 0.7 copy.24
  89.2 1.1 fusion.45
  90.5 58.9 %while.33 = (s32[]{:T(128)}, f32[64,4,128]{2,1,0:T(4,128)S(1)}, s32[]{:T(128)}, s32[8,4]{1,0:T(8,128)S(1)}, s32[8]{0:T(128)S(1)}, /*index=5*/bf16[32,128,128]{2,...) while((s32[]{:T(128)}, f32[64,4,128]{2,1,0:T(4,128)S(1)}, ...), condition=%wide.region_4.5_spmd, body=%wide.region_3.4_spmd.sunk | while | flops 8945742 | bytes 1245714 | solution.py:113
  90.8 1.1 fusion.130
  93.1 5.4 %collective-permute-done.1 = f32[64,4,128]{2,1,0:T(4,128)S(1)} collective-permute-done((f32[64,4,128]{2,1,0:T(4,128)S(1)}, f32[64,4,128]{2,1,0:T(4,128)S(1)}, u32[]{:S(2)}, u32[]{:S(2)}) %collective-permute-start.1) | collective-permute-done | bytes 131104 | tf_op jit(solution)/shard_map/while/body/eval_jaxpr/ppermute | solution.py:22
  99.2 1.1 fusion.130
  101.5 5.2 %collective-permute-done.1 = f32[64,4,128]{2,1,0:T(4,128)S(1)} collective-permute-done((f32[64,4,128]{2,1,0:T(4,128)S(1)}, f32[64,4,128]{2,1,0:T(4,128)S(1)}, u32[]{:S(2)}, u32[]{:S(2)}) %collective-permute-start.1) | collective-permute-done | bytes 131104 | tf_op jit(solution)/shard_map/while/body/eval_jaxpr/ppermute | solution.py:22
  107.4 1.1 fusion.130
  109.7 5.1 %collective-permute-done.1 = f32[64,4,128]{2,1,0:T(4,128)S(1)} collective-permute-done((f32[64,4,128]{2,1,0:T(4,128)S(1)}, f32[64,4,128]{2,1,0:T(4,128)S(1)}, u32[]{:S(2)}, u32[]{:S(2)}) %collective-permute-start.1) | collective-permute-done | bytes 131104 | tf_op jit(solution)/shard_map/while/body/eval_jaxpr/ppermute | solution.py:22
  115.6 1.1 fusion.130
  117.9 5.2 %collective-permute-done.1 = f32[64,4,128]{2,1,0:T(4,128)S(1)} collective-permute-done((f32[64,4,128]{2,1,0:T(4,128)S(1)}, f32[64,4,128]{2,1,0:T(4,128)S(1)}, u32[]{:S(2)}, u32[]{:S(2)}) %collective-permute-start.1) | collective-permute-done | bytes 131104 | tf_op jit(solution)/shard_map/while/body/eval_jaxpr/ppermute | solution.py:22
  123.7 1.1 fusion.130
  126.0 5.3 %collective-permute-done.1 = f32[64,4,128]{2,1,0:T(4,128)S(1)} collective-permute-done((f32[64,4,128]{2,1,0:T(4,128)S(1)}, f32[64,4,128]{2,1,0:T(4,128)S(1)}, u32[]{:S(2)}, u32[]{:S(2)}) %collective-permute-start.1) | collective-permute-done | bytes 131104 | tf_op jit(solution)/shard_map/while/body/eval_jaxpr/ppermute | solution.py:22
  132.1 1.1 fusion.130
  134.4 6.5 %collective-permute-done.1 = f32[64,4,128]{2,1,0:T(4,128)S(1)} collective-permute-done((f32[64,4,128]{2,1,0:T(4,128)S(1)}, f32[64,4,128]{2,1,0:T(4,128)S(1)}, u32[]{:S(2)}, u32[]{:S(2)}) %collective-permute-start.1) | collective-permute-done | bytes 131104 | tf_op jit(solution)/shard_map/while/body/eval_jaxpr/ppermute | solution.py:22
  141.7 1.1 fusion.130
  144.0 5.1 %collective-permute-done.1 = f32[64,4,128]{2,1,0:T(4,128)S(1)} collective-permute-done((f32[64,4,128]{2,1,0:T(4,128)S(1)}, f32[64,4,128]{2,1,0:T(4,128)S(1)}, u32[]{:S(2)}, u32[]{:S(2)}) %collective-permute-start.1) | collective-permute-done | bytes 131104 | tf_op jit(solution)/shard_map/while/body/eval_jaxpr/ppermute | solution.py:22
  150.1 60.2 %all-reduce.2.cloned.1.call-done = f32[256,256]{1,0:T(8,128)} async-done(((f32[256,256]{1,0:T(8,128)}), f32[256,256]{1,0:T(8,128)}) %all-reduce.2.cloned.1.call-update) | async-done | bytes 262160 | tf_op jit(solution)/shard_map/psum | solution.py:92
  210.3 1.7 copy.98
  (130 shorter events, 31.3 us)
Async XLA Ops:
  7.2 76.7 %copy-start = (bf16[256,256]{1,0:T(8,128)(2,1)S(1)}, bf16[256,256]{1,0:T(8,128)(2,1)}, u32[]{:S(2)}) copy-start(bf16[256,256]{1,0:T(8,128)(2,1)} %param.16) | copy-start | bytes 393220
  8.1 0.7 copy-start.3
  8.7 0.7 copy-start.2
  9.5 0.7 copy-start.4
  13.1 8.3 %collective-permute-start = (bf16[64,512]{1,0:T(8,128)(2,1)S(1)}, bf16[64,512]{1,0:T(8,128)(2,1)S(1)}, u32[]{:S(2)}, u32[]{:S(2)}) collective-permute-start(bf16[64,512]{1,0:T(8,128)(2,1)S(1)} %get-tuple-element.614), channel_id=1, source_target_pairs={{0,4},{4,8},{8,12},{12,16},{16,20},{20,24},{24,28},{28,0},{1,5},{5... | collective-permute-start | bytes 196616 | tf_op jit(solution)/shard_map/while/body/eval_jaxpr/ppermute | solution.py:22
  23.1 7.0 %collective-permute-start = (bf16[64,512]{1,0:T(8,128)(2,1)S(1)}, bf16[64,512]{1,0:T(8,128)(2,1)S(1)}, u32[]{:S(2)}, u32[]{:S(2)}) collective-permute-start(bf16[64,512]{1,0:T(8,128)(2,1)S(1)} %get-tuple-element.614), channel_id=1, source_target_pairs={{0,4},{4,8},{8,12},{12,16},{16,20},{20,24},{24,28},{28,0},{1,5},{5... | collective-permute-start | bytes 196616 | tf_op jit(solution)/shard_map/while/body/eval_jaxpr/ppermute | solution.py:22
  31.9 7.0 %collective-permute-start = (bf16[64,512]{1,0:T(8,128)(2,1)S(1)}, bf16[64,512]{1,0:T(8,128)(2,1)S(1)}, u32[]{:S(2)}, u32[]{:S(2)}) collective-permute-start(bf16[64,512]{1,0:T(8,128)(2,1)S(1)} %get-tuple-element.614), channel_id=1, source_target_pairs={{0,4},{4,8},{8,12},{12,16},{16,20},{20,24},{24,28},{28,0},{1,5},{5... | collective-permute-start | bytes 196616 | tf_op jit(solution)/shard_map/while/body/eval_jaxpr/ppermute | solution.py:22
  40.6 7.0 %collective-permute-start = (bf16[64,512]{1,0:T(8,128)(2,1)S(1)}, bf16[64,512]{1,0:T(8,128)(2,1)S(1)}, u32[]{:S(2)}, u32[]{:S(2)}) collective-permute-start(bf16[64,512]{1,0:T(8,128)(2,1)S(1)} %get-tuple-element.614), channel_id=1, source_target_pairs={{0,4},{4,8},{8,12},{12,16},{16,20},{20,24},{24,28},{28,0},{1,5},{5... | collective-permute-start | bytes 196616 | tf_op jit(solution)/shard_map/while/body/eval_jaxpr/ppermute | solution.py:22
  49.4 7.0 %collective-permute-start = (bf16[64,512]{1,0:T(8,128)(2,1)S(1)}, bf16[64,512]{1,0:T(8,128)(2,1)S(1)}, u32[]{:S(2)}, u32[]{:S(2)}) collective-permute-start(bf16[64,512]{1,0:T(8,128)(2,1)S(1)} %get-tuple-element.614), channel_id=1, source_target_pairs={{0,4},{4,8},{8,12},{12,16},{16,20},{20,24},{24,28},{28,0},{1,5},{5... | collective-permute-start | bytes 196616 | tf_op jit(solution)/shard_map/while/body/eval_jaxpr/ppermute | solution.py:22
  58.2 7.0 %collective-permute-start = (bf16[64,512]{1,0:T(8,128)(2,1)S(1)}, bf16[64,512]{1,0:T(8,128)(2,1)S(1)}, u32[]{:S(2)}, u32[]{:S(2)}) collective-permute-start(bf16[64,512]{1,0:T(8,128)(2,1)S(1)} %get-tuple-element.614), channel_id=1, source_target_pairs={{0,4},{4,8},{8,12},{12,16},{16,20},{20,24},{24,28},{28,0},{1,5},{5... | collective-permute-start | bytes 196616 | tf_op jit(solution)/shard_map/while/body/eval_jaxpr/ppermute | solution.py:22
  66.9 7.0 %collective-permute-start = (bf16[64,512]{1,0:T(8,128)(2,1)S(1)}, bf16[64,512]{1,0:T(8,128)(2,1)S(1)}, u32[]{:S(2)}, u32[]{:S(2)}) collective-permute-start(bf16[64,512]{1,0:T(8,128)(2,1)S(1)} %get-tuple-element.614), channel_id=1, source_target_pairs={{0,4},{4,8},{8,12},{12,16},{16,20},{20,24},{24,28},{28,0},{1,5},{5... | collective-permute-start | bytes 196616 | tf_op jit(solution)/shard_map/while/body/eval_jaxpr/ppermute | solution.py:22
  76.3 4.2 %copy-start.1 = (bf16[256,128]{1,0:T(8,128)(2,1)S(1)}, bf16[256,128]{1,0:T(8,128)(2,1)}, u32[]{:S(2)}) copy-start(bf16[256,128]{1,0:T(8,128)(2,1)} %param.17) | copy-start | bytes 196612
  76.3 7.5 %all-to-all-start = ((bf16[64,4,128]{2,0,1:T(8,128)(2,1)}), bf16[64,4,128]{2,0,1:T(8,128)(2,1)S(1)}, u32[]{:S(2)}, u32[]{:S(2)}) async-start(bf16[64,4,128]{2,0,1:T(8,128)(2,1)} %copy.70), calls=%async_computation | async-start | bytes 131072 | tf_op jit(solution)/shard_map/all_to_all | solution.py:82
  79.8 130.5 %all-reduce.2.cloned.1.call-start = ((), (), s32[]{:S(2)}) async-start(), calls=%async_computation.1 | async-start | bytes 524288 | tf_op jit(solution)/shard_map/psum | solution.py:92
  84.4 3.6 %collective-permute-start.4 = (bf16[64,128]{1,0:T(8,128)(2,1)S(1)}, bf16[64,128]{1,0:T(8,128)(2,1)S(1)}, u32[]{:S(2)}, u32[]{:S(2)}) collective-permute-start(bf16[64,128]{1,0:T(8,128)(2,1)S(1)} %get-tuple-element.485), channel_id=1, source_target_pairs={{0,3},{1,2},{2,1},{3,0},{4,7},{5,6},{6,5},{7,4},{8,11},{9,10},{10,... | collective-permute-start | bytes 49160 | tf_op jit(solution)/shard_map/ppermute | solution.py:100
  84.5 3.8 %collective-permute-start.3 = (bf16[64,128]{1,0:T(8,128)(2,1)S(1)}, bf16[64,128]{1,0:T(8,128)(2,1)S(1)}, u32[]{:S(2)}, u32[]{:S(2)}) collective-permute-start(bf16[64,128]{1,0:T(8,128)(2,1)S(1)} %get-tuple-element.486), channel_id=1, source_target_pairs={{0,2},{1,3},{2,0},{3,1},{4,6},{5,7},{6,4},{7,5},{8,10},{9,11},{10,... | collective-permute-start | bytes 49160 | tf_op jit(solution)/shard_map/ppermute | solution.py:100
  85.8 2.5 %collective-permute-start.2 = (bf16[64,128]{1,0:T(8,128)(2,1)S(1)}, bf16[64,128]{1,0:T(8,128)(2,1)S(1)}, u32[]{:S(2)}, u32[]{:S(2)}) collective-permute-start(bf16[64,128]{1,0:T(8,128)(2,1)S(1)} %get-tuple-element.487), channel_id=1, source_target_pairs={{0,1},{1,0},{2,3},{3,2},{4,5},{5,4},{6,7},{7,6},{8,9},{9,8},{10,11... | collective-permute-start | bytes 49160 | tf_op jit(solution)/shard_map/ppermute | solution.py:100
  90.5 8.0 %collective-permute-start.1 = (f32[64,4,128]{2,1,0:T(4,128)S(1)}, f32[64,4,128]{2,1,0:T(4,128)S(1)}, u32[]{:S(2)}, u32[]{:S(2)}) collective-permute-start(f32[64,4,128]{2,1,0:T(4,128)S(1)} %get-tuple-element.656), channel_id=1, source_target_pairs={{0,4},{4,8},{8,12},{12,16},{16,20},{20,24},{24,28},{28,0},{1,5},{5... | collective-permute-start | bytes 393224 | tf_op jit(solution)/shard_map/while/body/eval_jaxpr/ppermute | solution.py:22
  98.8 7.9 %collective-permute-start.1 = (f32[64,4,128]{2,1,0:T(4,128)S(1)}, f32[64,4,128]{2,1,0:T(4,128)S(1)}, u32[]{:S(2)}, u32[]{:S(2)}) collective-permute-start(f32[64,4,128]{2,1,0:T(4,128)S(1)} %get-tuple-element.656), channel_id=1, source_target_pairs={{0,4},{4,8},{8,12},{12,16},{16,20},{20,24},{24,28},{28,0},{1,5},{5... | collective-permute-start | bytes 393224 | tf_op jit(solution)/shard_map/while/body/eval_jaxpr/ppermute | solution.py:22
  107.1 7.8 %collective-permute-start.1 = (f32[64,4,128]{2,1,0:T(4,128)S(1)}, f32[64,4,128]{2,1,0:T(4,128)S(1)}, u32[]{:S(2)}, u32[]{:S(2)}) collective-permute-start(f32[64,4,128]{2,1,0:T(4,128)S(1)} %get-tuple-element.656), channel_id=1, source_target_pairs={{0,4},{4,8},{8,12},{12,16},{16,20},{20,24},{24,28},{28,0},{1,5},{5... | collective-permute-start | bytes 393224 | tf_op jit(solution)/shard_map/while/body/eval_jaxpr/ppermute | solution.py:22
  115.2 7.8 %collective-permute-start.1 = (f32[64,4,128]{2,1,0:T(4,128)S(1)}, f32[64,4,128]{2,1,0:T(4,128)S(1)}, u32[]{:S(2)}, u32[]{:S(2)}) collective-permute-start(f32[64,4,128]{2,1,0:T(4,128)S(1)} %get-tuple-element.656), channel_id=1, source_target_pairs={{0,4},{4,8},{8,12},{12,16},{16,20},{20,24},{24,28},{28,0},{1,5},{5... | collective-permute-start | bytes 393224 | tf_op jit(solution)/shard_map/while/body/eval_jaxpr/ppermute | solution.py:22
  123.4 8.0 %collective-permute-start.1 = (f32[64,4,128]{2,1,0:T(4,128)S(1)}, f32[64,4,128]{2,1,0:T(4,128)S(1)}, u32[]{:S(2)}, u32[]{:S(2)}) collective-permute-start(f32[64,4,128]{2,1,0:T(4,128)S(1)} %get-tuple-element.656), channel_id=1, source_target_pairs={{0,4},{4,8},{8,12},{12,16},{16,20},{20,24},{24,28},{28,0},{1,5},{5... | collective-permute-start | bytes 393224 | tf_op jit(solution)/shard_map/while/body/eval_jaxpr/ppermute | solution.py:22
  131.7 9.2 %collective-permute-start.1 = (f32[64,4,128]{2,1,0:T(4,128)S(1)}, f32[64,4,128]{2,1,0:T(4,128)S(1)}, u32[]{:S(2)}, u32[]{:S(2)}) collective-permute-start(f32[64,4,128]{2,1,0:T(4,128)S(1)} %get-tuple-element.656), channel_id=1, source_target_pairs={{0,4},{4,8},{8,12},{12,16},{16,20},{20,24},{24,28},{28,0},{1,5},{5... | collective-permute-start | bytes 393224 | tf_op jit(solution)/shard_map/while/body/eval_jaxpr/ppermute | solution.py:22
  141.3 7.7 %collective-permute-start.1 = (f32[64,4,128]{2,1,0:T(4,128)S(1)}, f32[64,4,128]{2,1,0:T(4,128)S(1)}, u32[]{:S(2)}, u32[]{:S(2)}) collective-permute-start(f32[64,4,128]{2,1,0:T(4,128)S(1)} %get-tuple-element.656), channel_id=1, source_target_pairs={{0,4},{4,8},{8,12},{12,16},{16,20},{20,24},{24,28},{28,0},{1,5},{5... | collective-permute-start | bytes 393224 | tf_op jit(solution)/shard_map/while/body/eval_jaxpr/ppermute | solution.py:22
Sparse Core Ops, SparseCore 0:
  88.1 122.0 all-reduce.1
